TPU v7x, 32 devices: a whole 2x2x4 slice. The times are simulated.
32 devices in a mesh: section: 4 (over x, core), sp: 8 (over z, y).
Axes of the slice: x: 2, y: 2, z: 4, core: 2. Of those that a mesh axis runs over, the one named last changes fastest.
Arguments:
- field_in: bfloat16 [4, 384, 192, 768], P('section', 'sp'), may hold values from -6 to 6
- spectral_gain: bfloat16 [4, 192], P('section'), may hold values from 0.5 to 1.5
- spectral_weight: bfloat16 [4, 384, 192, 384], P('section', 'sp'), may hold values from -0.3125 to 0.3125
- mixer_gain: bfloat16 [4, 192], P('section'), may hold values from 0.5 to 1.5
- up_weight: bfloat16 [4, 192, 384], P('section'), may hold values from -0.4375 to 0.4375
- up_bias: bfloat16 [4, 384], P('section'), may hold values from -3 to 3
- down_weight: bfloat16 [4, 192, 384], P('section'), may hold values from -0.3125 to 0.3125
Outputs:
- next_field: bfloat16 [4, 384, 192, 768], P('section', 'sp')
All inputs are finite; a program needn't handle non-finite values.
Results may differ from a plain program's by a relative error of at most 0.012.
Values may be sent and summed in bfloat16 or wider, within the bound.
A program may use at most 192 MiB of HBM per device.

v0:
```python
import math

import jax
import jax.numpy as jnp
from jax import lax
from jax.sharding import PartitionSpec as P

C = 192
NLAT = 384
NLON = 768
LMAX = 384
MMAX = 384


EPSILON = 1e-05


def passed_along(value, axis, by):
    count = lax.axis_size(axis)
    return lax.ppermute(value, axis, [(i, (i + by) % count) for i in range(count)])


def quad_weights(cycle_index, cycle_count):
    terms_count = cycle_count // 2
    orders = jnp.arange(1, terms_count + 1, dtype=jnp.int32)
    phase_turns = orders[None, :] * (2 * cycle_index[:, None] + 1) % (2 * cycle_count)
    angles = math.pi * phase_turns.astype(jnp.float32) / cycle_count
    orders_real = orders.astype(jnp.float32)
    series = jnp.sum(jnp.cos(angles) / (4.0 * orders_real * orders_real - 1.0)[None, :], axis=1)
    return 2.0 / cycle_count * (1.0 - 2.0 * series)


def fourier_tables(point_count, orders):
    points = jnp.arange(point_count, dtype=jnp.int32)
    phase_turns = points[:, None] * orders[None, :] % point_count
    angles = 2.0 * math.pi / point_count * phase_turns.astype(jnp.float32)
    cosines = jnp.cos(angles)
    sine_values = jnp.sin(angles)
    forward = jnp.stack([cosines, -sine_values], axis=1).astype(jnp.bfloat16)
    doubling = jnp.where(orders == 0, 1.0, 2.0).astype(jnp.float32)[:, None]
    inverse = jnp.stack([cosines.T * doubling, -sine_values.T * doubling], axis=0).astype(
        jnp.bfloat16
    )
    return (forward, inverse)


def step_entries(degree, order_col, cosines):
    active = degree >= order_col + 1.0
    further = degree >= order_col + 2.0
    degree_sq = degree * degree
    order_sq = order_col * order_col
    lead_coeff = jnp.sqrt(
        jnp.where(
            active, (4.0 * degree_sq - 1.0) / jnp.where(active, degree_sq - order_sq, 1.0), 0.0
        )
    )
    before = degree - 1.0
    before_sq = before * before
    trail_coeff = jnp.sqrt(
        jnp.where(
            further, (before_sq - order_sq) / jnp.where(further, 4.0 * before_sq - 1.0, 1.0), 0.0
        )
    )
    diag_top = jnp.where(active, lead_coeff * cosines, 1.0)
    off_top = jnp.where(active, -lead_coeff * trail_coeff, 0.0)
    off_low = jnp.where(active, 1.0, 0.0)
    diag_low = jnp.where(active, 0.0, 1.0)
    return (diag_top, off_top, off_low, diag_low)


def legendre_rows(order_index, cycle_count, degree_count):
    colatitude = math.pi * (jnp.arange(cycle_count, dtype=jnp.float32) + 0.5) / cycle_count
    cosines = jnp.cos(colatitude)[None, None, :]
    sine_values = jnp.sin(colatitude)
    order_real = order_index.astype(jnp.float32)
    steps_all = jnp.arange(1, degree_count + 1, dtype=jnp.float32)
    factors = jnp.log((2.0 * steps_all - 1.0) / (2.0 * steps_all))
    below_mask = (steps_all[None, :] <= order_real[:, None]).astype(jnp.float32)
    partial_log = jnp.sum(below_mask * factors[None, :], axis=1)
    start_log = 0.5 * jnp.log((2.0 * order_real + 1.0) / (4.0 * math.pi)) + 0.5 * partial_log
    start_log = start_log[:, None] + order_real[:, None] * jnp.log(sine_values)[None, :]
    order_col = order_real[None, :, None]
    block_count = degree_count // 16
    block_base = (16 * jnp.arange(block_count, dtype=jnp.int32)).astype(jnp.float32)[:, None, None]
    shape_all = (block_count, order_index.shape[0], cycle_count)
    unit_array = jnp.ones(shape_all, jnp.float32)
    zero_array = jnp.zeros(shape_all, jnp.float32)

    def product_half(half_turn, matrices):
        upper_left, upper_right, lower_left, lower_right, log_scale = matrices
        for inner_step in range(8):
            degree = block_base + (half_turn * 8 + inner_step).astype(jnp.float32)
            diag_top, off_top, off_low, diag_low = step_entries(degree, order_col, cosines)
            next_ul = diag_top * upper_left + off_top * lower_left
            next_ur = diag_top * upper_right + off_top * lower_right
            next_ll = off_low * upper_left + diag_low * lower_left
            next_lr = off_low * upper_right + diag_low * lower_right
            largest = jnp.maximum(
                jnp.maximum(jnp.abs(next_ul), jnp.abs(next_ur)),
                jnp.maximum(jnp.abs(next_ll), jnp.abs(next_lr)),
            )
            upper_left = next_ul / largest
            upper_right = next_ur / largest
            lower_left = next_ll / largest
            lower_right = next_lr / largest
            log_scale = log_scale + jnp.log(largest)
        return (upper_left, upper_right, lower_left, lower_right, log_scale)

    products = lax.fori_loop(
        0, 2, product_half, (unit_array, zero_array, zero_array, unit_array, zero_array)
    )

    def carry_block(vector_state, block_matrix):
        lead_value, lag_value, log_value = vector_state
        upper_left, upper_right, lower_left, lower_right, log_scale = block_matrix
        next_lead = upper_left * lead_value + upper_right * lag_value
        next_lag = lower_left * lead_value + lower_right * lag_value
        largest = jnp.maximum(jnp.abs(next_lead), jnp.abs(next_lag))
        return (
            (next_lead / largest, next_lag / largest, log_value + log_scale + jnp.log(largest)),
            vector_state,
        )

    initial = (unit_array[0], zero_array[0], start_log)
    final_state, starts = lax.scan(carry_block, initial, products)

    def degree_half(vector_state, half_turn):
        lead_value, lag_value, log_value = vector_state
        values = []
        for inner_step in range(8):
            degree = block_base + (half_turn * 8 + inner_step).astype(jnp.float32)
            diag_top, off_top, off_low, diag_low = step_entries(degree, order_col, cosines)
            next_lead = diag_top * lead_value + off_top * lag_value
            next_lag = off_low * lead_value + diag_low * lag_value
            largest = jnp.maximum(jnp.abs(next_lead), jnp.abs(next_lag))
            lead_value = next_lead / largest
            lag_value = next_lag / largest
            log_value = log_value + jnp.log(largest)
            values.append(lead_value * jnp.exp(log_value))
        return ((lead_value, lag_value, log_value), jnp.stack(values))

    last_state, table_rows = lax.scan(degree_half, starts, jnp.arange(2, dtype=jnp.int32))
    legendre = jnp.transpose(table_rows, (3, 2, 0, 1, 4)).reshape(
        order_index.shape[0], degree_count, cycle_count
    )
    degrees = jnp.arange(degree_count, dtype=jnp.int32)
    return jnp.where(degrees[None, :, None] >= order_index[:, None, None], legendre, 0.0)


def layer_norm(values, gain_row):
    values = values.astype(jnp.float32)
    average = jnp.mean(values, axis=-2, keepdims=True)
    centred = values - average
    variance = jnp.mean(centred * centred, axis=-2, keepdims=True)
    return centred * lax.rsqrt(variance + EPSILON) * gain_row.astype(jnp.float32)[:, None]


def mixing_matrix(weight):
    width = weight.shape[1]
    real_weight = weight[:, :, :width]
    imag_weight = weight[:, :, width:]
    top_half = jnp.concatenate([real_weight, imag_weight], axis=2)
    bottom_half = jnp.concatenate([-imag_weight, real_weight], axis=2)
    return jnp.concatenate([top_half, bottom_half], axis=1)


def order_list(sp_count, modes_dev):
    slots = jnp.arange(MMAX, dtype=jnp.int32)
    owner = slots // modes_dev
    within = slots % modes_dev
    mirrored = jnp.where(within % 2 == 0, owner, sp_count - 1 - owner)
    return within * sp_count + mirrored


def shards(field_in, spectral_gain, spectral_weight, mixer_gain, up_weight, up_bias, down_weight):
    grid_values = field_in[0]
    cycle_rows = grid_values.shape[0]
    sp_count = lax.axis_size("sp")
    device_rank = lax.axis_index("sp")
    modes_dev = MMAX // sp_count
    all_orders = order_list(sp_count, modes_dev)
    order_index = lax.dynamic_slice_in_dim(all_orders, device_rank * modes_dev, modes_dev, 0)
    cycle_index = device_rank * cycle_rows + jnp.arange(cycle_rows, dtype=jnp.int32)
    legendre = legendre_rows(order_index, NLAT, LMAX).astype(jnp.bfloat16)
    forward, inverse = fourier_tables(NLON, all_orders)
    weighting = quad_weights(cycle_index, NLAT) * (2.0 * math.pi / NLON)
    normed = layer_norm(grid_values, spectral_gain[0]).astype(jnp.bfloat16)
    spectral = jnp.einsum("nrm,acn->marc", forward, normed, preferred_element_type=jnp.float32)
    spectral = (
        (spectral * weighting[None, :, None, None])
        .astype(jnp.bfloat16)
        .reshape(MMAX, cycle_rows, 2 * C)
    )
    coeffs = jnp.einsum(
        "mla,mak->mlk",
        legendre,
        lax.all_to_all(spectral, "sp", split_axis=0, concat_axis=1, tiled=True),
        preferred_element_type=jnp.float32,
    ).astype(jnp.bfloat16)
    by_degree = lax.all_to_all(coeffs, "sp", split_axis=1, concat_axis=0, tiled=True)
    block_weight = mixing_matrix(spectral_weight[0])
    mixed_coeffs = jnp.einsum(
        "mlk,lkj->mlj", by_degree, block_weight, preferred_element_type=jnp.float32
    ).astype(jnp.bfloat16)
    grid_part = jnp.einsum(
        "mla,mlk->mak",
        legendre,
        lax.all_to_all(mixed_coeffs, "sp", split_axis=0, concat_axis=1, tiled=True),
        preferred_element_type=jnp.float32,
    ).astype(jnp.bfloat16)
    on_grid = lax.all_to_all(grid_part, "sp", split_axis=1, concat_axis=0, tiled=True)
    synthesis = jnp.einsum(
        "marc,rmn->acn",
        on_grid.reshape(MMAX, cycle_rows, 2, C),
        inverse,
        preferred_element_type=jnp.float32,
    )
    residual = grid_values.astype(jnp.float32) + synthesis
    hidden_in = layer_norm(residual, mixer_gain[0]).astype(jnp.bfloat16)
    hidden = jnp.einsum(
        "acn,ch->anh", hidden_in, up_weight[0], preferred_element_type=jnp.float32
    ) + up_bias[0].astype(jnp.float32)
    hidden = jax.nn.gelu(hidden, approximate=False).astype(jnp.bfloat16)
    branch = jnp.einsum("anh,ch->acn", hidden, down_weight[0], preferred_element_type=jnp.float32)
    result = (residual + branch).astype(jnp.bfloat16)
    received = passed_along(result, "section", 1)
    return received[None]


def solution(mesh):
    in_specs = (
        P("section", "sp", None, None),
        P("section", None),
        P("section", "sp", None, None),
        P("section", None),
        P("section", None, None),
        P("section", None),
        P("section", None, None),
    )
    out_specs = P("section", "sp", None, None)
    return jax.shard_map(shards, mesh=mesh, in_specs=in_specs, out_specs=out_specs, check_vma=False)
```

profile of v0, /device:TPU:0, one launch (start us, length us, event | category | flops | bytes accessed | tf_op | source)
XLA Modules:
  0.0 1913.3 jit_solution(2822400345149192253)
XLA Ops:
  0.1 5.1 cosine_convert_fusion
  5.5 7.8 convert_reduce_fusion
  13.4 10.3 fusion.194
  23.7 19.1 %multiply_convert_fusion.1 = bf16[48,192,2,384]{3,1,2,0:T(8,128)(2,1)} fusion(f32[48]{0:T(128)S(1)} %subtract_multiply_fusion, bf16[1,48,192,768]{3,2,1,0:T(8,128)(2,1)} %param.13, f32[192]{0:T(256)S(1)} %bitcast.468, f32[48,768]{1,0:T(8,128)S(1)} %add_rsqrt_fusion.1, f32[48,768]{1,0:T(8,128)S(1)} %broadcast_multiply_fusion.1, ...), kind=kOutput, calls=%fused_computation.509 | convolution fusion | flops 10923540480 | bytes 29787072 | tf_op jit(solution)/shard_map/nrm,acn->marc/dot_general | solution.py:188
  42.8 18.6 copy.38
  61.4 7.3 all-to-all-start
  71.0 60.1 %while.70 = (s32[]{:T(128)}, f32[24,48,384]{2,1,0:T(8,128)}, f32[24,48,384]{2,1,0:T(8,128)}, f32[24,48,384]{2,1,0:T(8,128)}, f32[24,48,384]{2,1,0:T(8,128)}, /*i...) while((s32[]{:T(128)}, f32[24,48,384]{2,1,0:T(8,128)}, ...), condition=%wide.region_2.3_spmd.clone.clone, body=%wide.region_1.2_spmd.clone.clone.sunk | while | flops 123129520 | bytes 200388496 | solution.py:109
  76.4 3.7 fusion.366
  81.4 3.7 fusion.368
  86.7 4.3 maximum_maximum_fusion.16
  91.0 4.7 fusion.370
  95.8 4.0 fusion.371
  100.2 5.7 fusion.364
  107.8 3.7 fusion.366
  112.8 3.7 fusion.368
  118.1 4.3 maximum_maximum_fusion.16
  122.4 4.7 fusion.370
  127.2 4.0 fusion.371
  131.3 58.0 %while.69 = (s32[]{:T(128)}, f32[48,384]{1,0:T(8,128)S(1)}, f32[48,384]{1,0:T(8,128)S(1)}, f32[48,384]{1,0:T(8,128)S(1)}, f32[24,48,384]{2,1,0:T(8,128)}, /*inde...) while((s32[]{:T(128)}, f32[48,384]{1,0:T(8,128)S(1)}, ...), condition=%wide.region_4.5_spmd.clone, body=%wide.region_3.4_spmd.clone.sunk | while | flops 368643 | bytes 1549461 | solution.py:125
  189.3 100.5 %while.68 = (s32[]{:T(128)}, f32[24,48,384]{2,1,0:T(8,128)}, f32[24,48,384]{2,1,0:T(8,128)}, f32[24,48,384]{2,1,0:T(8,128)S(1)}, bf16[2,8,24,48,384]{4,1,0,2,3:T...) while((s32[]{:T(128)}, f32[24,48,384]{2,1,0:T(8,128)}, ...), condition=%wide.region_6.7_spmd.clone.clone, body=%wide.region_5.6_spmd.clone.clone.sunk | while | flops 100568752 | bytes 101661032 | solution.py:142
  191.4 3.6 bitcast_dynamic-update-slice_fusion.21
  195.3 2.2 bitcast_dynamic-update-slice_fusion.22
  197.7 6.1 bitcast_dynamic-update-slice_fusion.23
  203.8 6.5 bitcast_dynamic-update-slice_fusion.24
  210.3 7.1 bitcast_dynamic-update-slice_fusion.25
  219.7 7.2 bitcast_dynamic-update-slice_fusion.27
  226.9 3.2 bitcast_dynamic-update-slice_fusion.28
  230.1 7.2 copy_dynamic-update-slice_fusion.2
  237.2 2.6 fusion.356
  241.5 3.6 bitcast_dynamic-update-slice_fusion.21
  245.3 2.2 bitcast_dynamic-update-slice_fusion.22
  247.7 6.1 bitcast_dynamic-update-slice_fusion.23
  253.8 6.5 bitcast_dynamic-update-slice_fusion.24
  260.4 7.1 bitcast_dynamic-update-slice_fusion.25
  269.7 7.2 bitcast_dynamic-update-slice_fusion.27
  276.9 3.2 bitcast_dynamic-update-slice_fusion.28
  280.1 7.2 copy_dynamic-update-slice_fusion.2
  287.2 2.6 fusion.356
  289.8 14.3 fusion.197
  304.1 71.4 %all-to-all-done = bf16[384,48,384]{2,1,0:T(8,128)(2,1)} async-done(((bf16[384,48,384]{2,1,0:T(8,128)(2,1)}), bf16[384,48,384]{2,1,0:T(8,128)(2,1)}, u32[]{:S(2)}, u32[]{:S(2)}) %all-to-all-start) | async-done | bytes 14155808 | tf_op jit(solution)/shard_map/all_to_all | solution.py:197
  375.5 12.9 copy.39
  388.4 19.4 %convolution_convert_fusion.1 = bf16[48,384,384]{2,1,0:T(8,128)(2,1)} fusion(bf16[48,384,384]{2,1,0:T(8,128)(2,1)} %fusion.197, bf16[48,384,384]{2,1,0:T(8,128)(2,1)} %bitcast.453), kind=kOutput, calls=%fused_computation.531 | convolution fusion | flops 5442895872 | bytes 42467328 | tf_op jit(solution)/shard_map/mla,mak->mlk/dot_general | solution.py:194
  407.8 31.5 %copy.40 = bf16[48,384,384]{2,0,1:T(8,128)(2,1)} copy(bf16[48,384,384]{2,1,0:T(8,128)(2,1)} %convolution_convert_fusion.1) | data formatting | bytes 28311552 | tf_op jit(solution)/shard_map/convert_element_type | solution.py:199
  439.3 5.5 all-to-all-start.1
  444.9 11.3 copy.37
  456.1 8.1 slice_negate_fusion
  464.2 286.5 %all-to-all-done.1 = bf16[48,384,384]{2,0,1:T(8,128)(2,1)} async-done(((bf16[48,384,384]{2,0,1:T(8,128)(2,1)}), bf16[48,384,384]{2,0,1:T(8,128)(2,1)}, u32[]{:S(2)}, u32[]{:S(2)}) %all-to-all-start.1) | async-done | bytes 14155808 | tf_op jit(solution)/shard_map/all_to_all | solution.py:200
  750.7 13.2 copy.41
  763.9 18.3 convert_bitcast_fusion.1
  782.2 18.4 copy.42
  800.6 311.4 %all_to_all.69 = bf16[384,48,384]{2,1,0:T(8,128)(2,1)S(1)} all-to-all(bf16[384,48,384]{2,1,0:T(8,128)(2,1)} %copy.42), channel_id=1, replica_groups=mesh['section'=4,'sp'=8] {'sp'}, dimensions={0} | all-to-all | bytes 28311552 | tf_op jit(solution)/shard_map/all_to_all | solution.py:208
  1112.0 6.0 copy.43
  1118.0 19.3 %convolution_convert_fusion = bf16[48,384,384]{2,1,0:T(8,128)(2,1)} fusion(bf16[48,384,384]{2,1,0:T(8,128)(2,1)} %fusion.197, bf16[48,384,384]{2,1,0:T(8,128)(2,1)} %bitcast.452), kind=kOutput, calls=%fused_computation.530 | convolution fusion | flops 5442895872 | bytes 42467328 | tf_op jit(solution)/shard_map/mla,mlk->mak/dot_general | solution.py:205
  1137.2 31.5 %copy.45 = bf16[48,384,384]{2,0,1:T(8,128)(2,1)} copy(bf16[48,384,384]{2,1,0:T(8,128)(2,1)} %convolution_convert_fusion) | data formatting | bytes 28311552 | tf_op jit(solution)/shard_map/convert_element_type | solution.py:210
  1168.8 5.6 all-to-all-start.3
  1174.5 5.5 multiply_convert_fusion.10
  1180.0 300.1 %all-to-all-done.3 = bf16[48,384,384]{2,0,1:T(8,128)(2,1)} async-done(((bf16[48,384,384]{2,0,1:T(8,128)(2,1)}), bf16[48,384,384]{2,0,1:T(8,128)(2,1)}, u32[]{:S(2)}, u32[]{:S(2)}) %all-to-all-start.3) | async-done | bytes 14155808 | tf_op jit(solution)/shard_map/all_to_all | solution.py:211
  1480.2 11.3 copy.67
  1491.5 39.4 %reshape.7003 = bf16[384,48,2,192]{3,2,1,0:T(2,128)(2,1)} reshape(bf16[8,48,48,384]{3,2,1,0:T(8,128)(2,1)} %bitcast.455) | data formatting | bytes 28311552 | tf_op jit(solution)/shard_map/reshape | solution.py:214
  1530.9 51.2 %fusion.319 = (f32[48,768]{1,0:T(8,128)S(1)}, f32[48,192,768]{2,1,0:T(8,128)}) fusion(bf16[1,384,768]{2,1,0:T(8,128)(2,1)S(1)} %get-tuple-element.1120, bf16[1,384,768]{2,1,0:T(8,128)(2,1)S(1)} %get-tuple-element.1119, bf16[384,48,2,192]{3,2,1,0:T(2,128)(2,1)} %reshape.7003, bf16[1,48,192,768]{3,2,1,0:T(8,128)(2,1)} %param.13), kind=kOutput, calls=%fused_computation.641 | convolution fusion | flops 10893422592 | bytes 57950208 | tf_op jit(solution)/shard_map/marc,rmn->acn/dot_general | solution.py:212
  1582.1 11.1 multiply_reduce_fusion
  1593.3 159.6 %fusion.198 = bf16[48,192,768]{2,1,0:T(8,128)(2,1)} fusion(f32[48,192,768]{2,1,0:T(8,128)} %get-tuple-element.1126, f32[384]{0:T(512)S(1)} %convert_reduce_fusion.1, f32[192]{0:T(256)S(1)} %bitcast.467, f32[48,768]{1,0:T(8,128)S(1)} %add_rsqrt_fusion, f32[48,768]{1,0:T(8,128)S(1)} %broadcast_multiply_fusion, bf16[1,192,384]{2,1,0:T(8,128)(2,1)S(1)} %copy-done, ...), kind=kOutput, calls=%fused_computation.506 | convolution fusion | flops 11848384512 | bytes 43059456 | tf_op jit(solution)/shard_map/anh,ch->acn/dot_general | solution.py:224
  1752.9 154.9 %collective-permute-done = bf16[48,192,768]{2,1,0:T(8,128)(2,1)S(1)} collective-permute-done((bf16[48,192,768]{2,1,0:T(8,128)(2,1)}, bf16[48,192,768]{2,1,0:T(8,128)(2,1)S(1)}, u32[]{:S(2)}, u32[]{:S(2)}) %collective-permute-start) | collective-permute-done | bytes 14155808 | tf_op jit(solution)/shard_map/ppermute | solution.py:20
  1907.8 5.3 copy.138
  (302 shorter events, 80.6 us)
Async XLA Ops:
  0.0 1593.3 %copy-start = (bf16[1,192,384]{2,1,0:T(8,128)(2,1)S(1)}, bf16[1,192,384]{2,1,0:T(8,128)(2,1)}, u32[]{:S(2)}) copy-start(bf16[1,192,384]{2,1,0:T(8,128)(2,1)} %param.19) | copy-start | bytes 442372
  0.0 69.4 %copy-start.12 = (s32[384]{0:T(512)}, s32[384]{0:T(512)S(1)}, u32[]{:S(2)}) copy-start(s32[384]{0:T(512)S(1)} %fusion.259) | copy-start | bytes 4612
  13.3 10.3 copy-start.18
  61.4 314.1 %all-to-all-start = ((bf16[384,48,384]{2,1,0:T(8,128)(2,1)}), bf16[384,48,384]{2,1,0:T(8,128)(2,1)}, u32[]{:S(2)}, u32[]{:S(2)}) async-start(bf16[384,48,384]{2,1,0:T(8,128)(2,1)} %copy.38), calls=%async_computation | async-start | bytes 28311552 | tf_op jit(solution)/shard_map/all_to_all | solution.py:197
  69.5 1.5 copy-start.15
  71.0 60.1 %copy-start.14 = (f32[384]{0:T(512)S(1)}, f32[384]{0:T(512)}, u32[]{:S(2)}) copy-start(f32[384]{0:T(512)} %sine_log_fusion) | copy-start | bytes 4612
  71.0 60.1 %copy-start.16 = (f32[48]{0:T(128)S(1)}, f32[48]{0:T(128)}, u32[]{:S(2)}) copy-start(f32[48]{0:T(128)} %copy-done.15) | copy-start | bytes 580
  71.0 60.1 %copy-start.20 = (f32[48]{0:T(128)S(1)}, f32[48]{0:T(128)}, u32[]{:S(2)}) copy-start(f32[48]{0:T(128)} %add_multiply_fusion.16) | copy-start | bytes 580
  71.0 60.2 %copy-start.1 = (f32[24,48,384]{2,1,0:T(8,128)S(1)}, f32[24,48,384]{2,1,0:T(8,128)}, u32[]{:S(2)}) copy-start(f32[24,48,384]{2,1,0:T(8,128)} %custom-call.11) | copy-start | bytes 5308420
  71.0 60.2 %copy-start.8 = (f32[48,384]{1,0:T(8,128)S(1)}, f32[48,384]{1,0:T(8,128)}, u32[]{:S(2)}) copy-start(f32[48,384]{1,0:T(8,128)} %custom-call) | copy-start | bytes 221188
  71.0 60.2 %copy-start.9 = (f32[48,384]{1,0:T(8,128)S(1)}, f32[48,384]{1,0:T(8,128)}, u32[]{:S(2)}) copy-start(f32[48,384]{1,0:T(8,128)} %custom-call.1) | copy-start | bytes 221188
  71.5 2.1 copy-start.2
  71.5 2.1 copy-start.3
  71.5 2.6 copy-start.4
  71.6 3.1 copy-start.5
  86.7 4.4 copy-start.6
  95.8 4.0 copy-start.7
  100.2 5.8 copy-start.2
  100.2 5.8 copy-start.3
  100.2 5.8 copy-start.4
  100.2 5.8 copy-start.5
  118.1 4.4 copy-start.6
  127.1 4.0 copy-start.7
  189.3 100.5 %copy-start.11 = (pred[48,384]{1,0:T(8,128)(4,1)S(1)}, pred[48,384]{1,0:T(8,128)(4,1)}, u32[]{:S(2)}) copy-start(pred[48,384]{1,0:T(8,128)(4,1)} %iota_compare_fusion) | copy-start | bytes 55300
  439.3 311.3 %all-to-all-start.1 = ((bf16[48,384,384]{2,0,1:T(8,128)(2,1)}), bf16[48,384,384]{2,0,1:T(8,128)(2,1)}, u32[]{:S(2)}, u32[]{:S(2)}) async-start(bf16[48,384,384]{2,0,1:T(8,128)(2,1)} %copy.40), calls=%async_computation.1 | async-start | bytes 28311552 | tf_op jit(solution)/shard_map/all_to_all | solution.py:200
  750.7 13.2 copy-start.10
  1168.8 5.7 copy-start.19
  1168.8 5.7 copy-start.17
  1168.8 5.7 copy-start.13
  1168.8 311.4 %all-to-all-start.3 = ((bf16[48,384,384]{2,0,1:T(8,128)(2,1)}), bf16[48,384,384]{2,0,1:T(8,128)(2,1)}, u32[]{:S(2)}, u32[]{:S(2)}) async-start(bf16[48,384,384]{2,0,1:T(8,128)(2,1)} %copy.45), calls=%async_computation.3 | async-start | bytes 28311552 | tf_op jit(solution)/shard_map/all_to_all | solution.py:211
  1582.1 11.2 copy-start.21
  1752.9 154.9 %collective-permute-start = (bf16[48,192,768]{2,1,0:T(8,128)(2,1)}, bf16[48,192,768]{2,1,0:T(8,128)(2,1)S(1)}, u32[]{:S(2)}, u32[]{:S(2)}) collective-permute-start(bf16[48,192,768]{2,1,0:T(8,128)(2,1)} %fusion.198), channel_id=1, source_target_pairs={{0,8},{8,16},{16,24},{24,0},{1,9},{9,17},{17,25},{25,1},{2,10},{10... | collective-permute-start | bytes 42467336 | tf_op jit(solution)/shard_map/ppermute | solution.py:20
where the time goes:
time: 1920 us; the launch traced here: 1910 us
  waiting for transfers between devices  813 us (42%)
  blocking collectives  311 us (16%)
  matrix products  287 us (15%)
  other arithmetic  264 us (14%)
  local copies, waits for them, and re-layouts  216 us (11%)
    all_to_all x1, blocking collectives, shards(): lax.all_to_all(mixed_coeffs, 'sp', split_axis=0, concat_axis=1, tiled=True)  311 us
    all_to_all x1, waiting for transfers between devices, shards(): lax.all_to_all(grid_part, 'sp', split_axis=1, concat_axis=0, tiled=True)  300 us
    all_to_all x1, waiting for transfers between devices, shards(): lax.all_to_all(coeffs, 'sp', split_axis=1, concat_axis=0, tiled=True)  287 us
    dot_general x1, matrix products, shards(): jnp.einsum('anh,ch->acn', hidden, down_weight[0], preferred_element_type=...  160 us
    ppermute x1, waiting for transfers between devices, passed_along(): lax.ppermute(value, axis, [(i, (i + by) % count) for i in range(count)])  155 us
    all_to_all x1, waiting for transfers between devices, shards(): lax.all_to_all(spectral, 'sp', split_axis=0, concat_axis=1, tiled=True)  71.4 us
    while x14, other arithmetic  69.9 us
    dot_general x1, matrix products, shards(): jnp.einsum('marc,rmn->acn', on_grid.reshape(MMAX, cycle_rows, 2, C), inve...  51.2 us
  transfers between devices with their start and end apart: 4, of which 4 were waited for; matrix products, arithmetic and copies ran while one was open for 13% of the time, Pallas kernels for 0%

commit v1 on v0

--- a/solution.py
+++ b/solution.py
@@ -10,6 +10,7 @@
 NLON = 768
 LMAX = 384
 MMAX = 384
+CHUNKS = 4
 
 
 EPSILON = 1e-05
@@ -172,6 +173,21 @@
     return within * sp_count + mirrored
 
 
+def triangle_plan(sp_count, half):
+    plan = []
+    for rank in range(sp_count):
+        low_block = min(rank, sp_count - 1 - rank)
+        high_block = sp_count - 1 - low_block
+        low_half = 0 if rank == low_block else 1
+        low_start = (2 * low_block + low_half) * half
+        high_start = (2 * high_block + 1 - low_half) * half
+        low_count = (low_start + half - 1) // sp_count + 1
+        high_count = (high_start + half - 1) // sp_count + 1
+        plan.append((low_start, low_count, high_start, high_count))
+    slots = max(entry[1] + entry[3] for entry in plan)
+    return (plan, slots)
+
+
 def shards(field_in, spectral_gain, spectral_weight, mixer_gain, up_weight, up_bias, down_weight):
     grid_values = field_in[0]
     cycle_rows = grid_values.shape[0]
@@ -197,34 +213,96 @@
         lax.all_to_all(spectral, "sp", split_axis=0, concat_axis=1, tiled=True),
         preferred_element_type=jnp.float32,
     ).astype(jnp.bfloat16)
-    by_degree = lax.all_to_all(coeffs, "sp", split_axis=1, concat_axis=0, tiled=True)
-    block_weight = mixing_matrix(spectral_weight[0])
-    mixed_coeffs = jnp.einsum(
-        "mlk,lkj->mlj", by_degree, block_weight, preferred_element_type=jnp.float32
-    ).astype(jnp.bfloat16)
-    grid_part = jnp.einsum(
-        "mla,mlk->mak",
-        legendre,
-        lax.all_to_all(mixed_coeffs, "sp", split_axis=0, concat_axis=1, tiled=True),
+    half = LMAX // sp_count // 2
+    plan, slots = triangle_plan(sp_count, half)
+    own_weight = spectral_weight[0]
+    partner = [(i, sp_count - 1 - i) for i in range(sp_count)]
+    other_weight = lax.ppermute(own_weight[half:], "sp", partner)
+    is_low = device_rank < sp_count // 2
+    low_weight = mixing_matrix(jnp.where(is_low, own_weight[:half], other_weight))
+    high_weight = mixing_matrix(jnp.where(is_low, other_weight, own_weight[:half]))
+    width = coeffs.shape[2]
+    pieces = []
+    for low_start, low_count, high_start, high_count in plan:
+        pieces.append(coeffs[:low_count, low_start : low_start + half])
+        gap = slots - low_count - high_count
+        if gap:
+            pieces.append(jnp.zeros((gap, half, width), coeffs.dtype))
+        pieces.append(coeffs[:high_count, high_start : high_start + half])
+    packed = jnp.concatenate(pieces, axis=0)
+    by_degree = lax.all_to_all(packed, "sp", split_axis=0, concat_axis=0, tiled=True)
+    by_degree = by_degree.reshape(sp_count, slots, half, width)
+    most_low = max(entry[1] for entry in plan)
+    most_high = max(entry[3] for entry in plan)
+    low_mixed = jnp.einsum(
+        "dslk,lkj->dslj",
+        by_degree[:, :most_low],
+        low_weight,
         preferred_element_type=jnp.float32,
     ).astype(jnp.bfloat16)
-    on_grid = lax.all_to_all(grid_part, "sp", split_axis=1, concat_axis=0, tiled=True)
-    synthesis = jnp.einsum(
-        "marc,rmn->acn",
-        on_grid.reshape(MMAX, cycle_rows, 2, C),
-        inverse,
+    high_mixed = jnp.einsum(
+        "dslk,lkj->dslj",
+        by_degree[:, slots - most_high :],
+        high_weight,
         preferred_element_type=jnp.float32,
-    )
-    residual = grid_values.astype(jnp.float32) + synthesis
-    hidden_in = layer_norm(residual, mixer_gain[0]).astype(jnp.bfloat16)
-    hidden = jnp.einsum(
-        "acn,ch->anh", hidden_in, up_weight[0], preferred_element_type=jnp.float32
-    ) + up_bias[0].astype(jnp.float32)
-    hidden = jax.nn.gelu(hidden, approximate=False).astype(jnp.bfloat16)
-    branch = jnp.einsum("anh,ch->acn", hidden, down_weight[0], preferred_element_type=jnp.float32)
-    result = (residual + branch).astype(jnp.bfloat16)
-    received = passed_along(result, "section", 1)
-    return received[None]
+    ).astype(jnp.bfloat16)
+    low_rows = jnp.array([entry[1] for entry in plan], jnp.int32)[device_rank]
+    row = jnp.arange(slots, dtype=jnp.int32)[None, :, None, None]
+    mixed = jnp.where(
+        row < low_rows,
+        jnp.pad(low_mixed, ((0, 0), (0, slots - most_low), (0, 0), (0, 0))),
+        jnp.pad(high_mixed, ((0, 0), (slots - most_high, 0), (0, 0), (0, 0))),
+    )
+    returned = lax.all_to_all(
+        mixed.reshape(sp_count * slots, half, width),
+        "sp",
+        split_axis=0,
+        concat_axis=0,
+        tiled=True,
+    ).reshape(sp_count, slots, half, width)
+    parts = {}
+    for rank, (low_start, low_count, high_start, high_count) in enumerate(plan):
+        parts[low_start] = (returned[rank, :low_count], low_count)
+        parts[high_start] = (returned[rank, slots - high_count :], high_count)
+    mixed_coeffs = jnp.concatenate(
+        [
+            jnp.pad(parts[start][0], ((0, modes_dev - parts[start][1]), (0, 0), (0, 0)))
+            for start in sorted(parts)
+        ],
+        axis=1,
+    )
+    grid_part = jnp.einsum(
+        "mla,mlk->mak", legendre, mixed_coeffs, preferred_element_type=jnp.float32
+    ).astype(jnp.bfloat16)
+    grid_part = grid_part.reshape(modes_dev, sp_count, cycle_rows, width)
+    chunk = cycle_rows // CHUNKS
+    outputs = []
+    for start in range(0, cycle_rows, chunk):
+        on_grid = lax.all_to_all(
+            grid_part[:, :, start : start + chunk].reshape(modes_dev, sp_count * chunk, width),
+            "sp",
+            split_axis=1,
+            concat_axis=0,
+            tiled=True,
+        )
+        synthesis = jnp.einsum(
+            "marc,rmn->acn",
+            on_grid.reshape(MMAX, chunk, 2, C),
+            inverse,
+            preferred_element_type=jnp.float32,
+        )
+        residual = grid_values[start : start + chunk].astype(jnp.float32) + synthesis
+        hidden_in = layer_norm(residual, mixer_gain[0]).astype(jnp.bfloat16)
+        hidden = jnp.einsum(
+            "acn,ch->anh", hidden_in, up_weight[0], preferred_element_type=jnp.float32
+        ) + up_bias[0].astype(jnp.float32)
+        hidden = jax.nn.gelu(hidden, approximate=False).astype(jnp.bfloat16)
+        branch = jnp.einsum(
+            "anh,ch->acn", hidden, down_weight[0], preferred_element_type=jnp.float32
+        )
+        result = (residual + branch).astype(jnp.bfloat16)
+        outputs.append(passed_along(result, "section", 1))
+    return jnp.concatenate(outputs, axis=0)[None]
 
 
 def solution(mesh):

time: 1920 us -> 1710 us (0.89)
  waiting for transfers between devices: 813 us -> 554 us
  blocking collectives: 311 us -> 253 us
  local copies, waits for them, and re-layouts: 216 us -> 264 us
  other arithmetic: 264 us -> 291 us
  starting transfers between devices: 18.5 us -> 37.7 us
    all_to_all x2 -> x5, waiting for transfers between devices: 587 us -> 246 us  [the longest x4 216 us: shards(): lax.all_to_all(grid_part[:, :, start:start + chunk].reshape(modes_dev, sp...]
    ppermute x0 -> x1, waiting for transfers between devices: none -> 191 us  [shards(): other_weight = lax.ppermute(own_weight[half:], 'sp', partner)]
    ppermute x1 -> x4, waiting for transfers between devices: 155 us -> 45.4 us  [passed_along(): lax.ppermute(value, axis, [(i, (i + by) % count) for i in range(count)])]
    convert_element_type x3 -> x0, local copies, waits for them, and re-layouts: 81.5 us -> none  [the longest x1 31.5 us: shards(): grid_part = jnp.einsum('mla,mlk->mak', legendre, lax.all_to_all(mixed_coe...]
    unnamed x34 -> x104, local copies, waits for them, and re-layouts: 16.6 us -> 87.1 us
    all_to_all x1, blocking collectives: 311 us -> 253 us  [shards(): lax.all_to_all(mixed.reshape(sp_count * slots, half, width), 'sp', split_...]
    reshape x1 -> x8, local copies, waits for them, and re-layouts: 39.4 us -> 90.3 us  [shards(): on_grid.reshape(MMAX, chunk, 2, C)]
    all_to_all x3 -> x0, local copies, waits for them, and re-layouts: 30.5 us -> none  [the longest x1 13.2 us: shards(): lax.all_to_all(coeffs, 'sp', split_axis=1, concat_axis=0, tiled=True)]
  transfers between devices with their start and end apart: 4 -> 11, of which waited for: 4 -> 8; matrix products, arithmetic and copies ran while one was open for 13% -> 27% of each run, Pallas kernels for 0% -> 0%
where the time goes in v1:
time: 1710 us; the launch traced here: 1700 us
  waiting for transfers between devices  554 us (32%)
  matrix products  298 us (17%)
  other arithmetic  291 us (17%)
  local copies, waits for them, and re-layouts  264 us (15%)
  blocking collectives  253 us (15%)
  starting transfers between devices  37.7 us (2%)
    all_to_all x1, blocking collectives, shards(): lax.all_to_all(mixed.reshape(sp_count * slots, half, width), 'sp', split_...  253 us
    all_to_all x4, waiting for transfers between devices, shards(): lax.all_to_all(grid_part[:, :, start:start + chunk].reshape(modes_dev, sp...  216 us
    ppermute x1, waiting for transfers between devices, shards(): other_weight = lax.ppermute(own_weight[half:], 'sp', partner)  191 us
    dot_general x4, matrix products, shards(): jnp.einsum('anh,ch->acn', hidden, down_weight[0], preferred_element_type=...  144 us
    reshape x8, local copies, waits for them, and re-layouts, shards(): on_grid.reshape(MMAX, chunk, 2, C)  90.3 us
    unnamed x104, local copies, waits for them, and re-layouts  87.1 us
    all_to_all x1, waiting for transfers between devices, shards(): lax.all_to_all(spectral, 'sp', split_axis=0, concat_axis=1, tiled=True)  71.5 us
    while x14, other arithmetic  69.9 us
  transfers between devices with their start and end apart: 11, of which 8 were waited for; matrix products, arithmetic and copies ran while one was open for 27% of the time, Pallas kernels for 0%

profile of v1, /device:TPU:0, one launch (start us, length us, event | category | flops | bytes accessed | tf_op | source)
XLA Modules:
  0.0 1701.2 jit_solution(16613426593756830060)
XLA Ops:
  1.2 7.8 convert_reduce_fusion
  9.0 10.3 fusion.183
  19.3 5.5 cosine_convert_fusion
  24.8 19.0 %multiply_convert_fusion = bf16[48,192,2,384]{3,1,2,0:T(8,128)(2,1)} fusion(f32[48]{0:T(128)S(1)} %subtract_multiply_fusion, bf16[1,48,192,768]{3,2,1,0:T(8,128)(2,1)} %param.14, f32[192]{0:T(256)S(1)} %bitcast.620, f32[48,768]{1,0:T(8,128)S(1)} %add_rsqrt_fusion, f32[48,768]{1,0:T(8,128)S(1)} %broadcast_multiply_fusion, ...), kind=kOutput, calls=%fused_computation.485 | convolution fusion | flops 10923540480 | bytes 29787072 | tf_op jit(solution)/shard_map/nrm,acn->marc/dot_general | solution.py:204
  43.8 18.6 %copy.34 = bf16[384,48,384]{2,1,0:T(8,128)(2,1)} copy(bf16[384,48,384]{0,2,1:T(8,128)(2,1)} %bitcast.601) | data formatting | bytes 28311552 | tf_op jit(solution)/shard_map/reshape | solution.py:208
  62.4 7.3 all-to-all-start
  72.0 59.7 %while.70 = (s32[]{:T(128)}, f32[24,48,384]{2,1,0:T(8,128)}, f32[24,48,384]{2,1,0:T(8,128)}, f32[24,48,384]{2,1,0:T(8,128)}, f32[24,48,384]{2,1,0:T(8,128)}, /*i...) while((s32[]{:T(128)}, f32[24,48,384]{2,1,0:T(8,128)}, ...), condition=%wide.region_2.3_spmd.clone.clone, body=%wide.region_1.2_spmd.clone.clone.sunk | while | flops 123129520 | bytes 200388496 | solution.py:110
  101.5 5.5 fusion.531
  132.4 58.0 %while.69 = (s32[]{:T(128)}, f32[48,384]{1,0:T(8,128)S(1)}, f32[48,384]{1,0:T(8,128)S(1)}, f32[48,384]{1,0:T(8,128)S(1)}, f32[24,48,384]{2,1,0:T(8,128)}, /*inde...) while((s32[]{:T(128)}, f32[48,384]{1,0:T(8,128)S(1)}, ...), condition=%wide.region_4.5_spmd.clone, body=%wide.region_3.4_spmd.clone.sunk | while | flops 368643 | bytes 1548453 | solution.py:126
  190.5 100.2 %while.68 = (s32[]{:T(128)}, f32[24,48,384]{2,1,0:T(8,128)}, f32[24,48,384]{2,1,0:T(8,128)}, f32[24,48,384]{2,1,0:T(8,128)S(1)}, bf16[2,8,24,48,384]{4,1,0,2,3:T...) while((s32[]{:T(128)}, f32[24,48,384]{2,1,0:T(8,128)}, ...), condition=%wide.region_6.7_spmd.clone.clone, body=%wide.region_5.6_spmd.clone.clone.sunk | while | flops 100568752 | bytes 101660528 | solution.py:143
  198.7 6.1 bitcast_dynamic-update-slice_fusion.23
  204.8 6.5 bitcast_dynamic-update-slice_fusion.24
  211.3 7.1 bitcast_dynamic-update-slice_fusion.25
  220.7 7.1 bitcast_dynamic-update-slice_fusion.27
  233.5 7.2 copy_dynamic-update-slice_fusion.2
  248.7 6.1 bitcast_dynamic-update-slice_fusion.23
  254.8 6.5 bitcast_dynamic-update-slice_fusion.24
  261.3 7.1 bitcast_dynamic-update-slice_fusion.25
  270.7 7.1 bitcast_dynamic-update-slice_fusion.27
  283.5 7.2 copy_dynamic-update-slice_fusion.2
  290.7 14.3 fusion.186
  305.0 71.5 %all-to-all-done = bf16[384,48,384]{2,1,0:T(8,128)(2,1)} async-done(((bf16[384,48,384]{2,1,0:T(8,128)(2,1)}), bf16[384,48,384]{2,1,0:T(8,128)(2,1)}, u32[]{:S(2)}, u32[]{:S(2)}) %all-to-all-start) | async-done | bytes 14155808 | tf_op jit(solution)/shard_map/all_to_all | solution.py:213
  376.5 12.9 copy.35
  389.4 19.7 %convolution_convert_fusion.1 = bf16[48,384,384]{2,1,0:T(8,128)(2,1)} fusion(bf16[48,384,384]{2,1,0:T(8,128)(2,1)} %fusion.186, bf16[48,384,384]{2,1,0:T(8,128)(2,1)} %bitcast.579), kind=kOutput, calls=%fused_computation.578 | convolution fusion | flops 5442895872 | bytes 42467328 | tf_op jit(solution)/shard_map/mla,mak->mlk/dot_general | solution.py:210
  453.3 191.3 %collective-permute-done = bf16[24,192,384]{2,1,0:T(8,128)(2,1)} collective-permute-done((bf16[24,192,384]{2,1,0:T(8,128)(2,1)}, bf16[24,192,384]{2,1,0:T(8,128)(2,1)}, u32[]{:S(2)}, u32[]{:S(2)}) %collective-permute-start) | collective-permute-done | bytes 3538976 | tf_op jit(solution)/shard_map/ppermute | solution.py:220
  655.4 29.7 %all-to-all-done.1 = bf16[408,24,384]{2,1,0:T(8,128)(2,1)} async-done(((bf16[408,24,384]{2,1,0:T(8,128)(2,1)}), bf16[408,24,384]{2,1,0:T(8,128)(2,1)}, u32[]{:S(2)}, u32[]{:S(2)}) %all-to-all-start.1) | async-done | bytes 7520288 | tf_op jit(solution)/shard_map/all_to_all | solution.py:233
  697.1 15.2 fusion.237
  712.3 8.9 convert_bitcast_fusion.1
  724.2 5.2 fusion.231
  731.8 12.0 pad_select_fusion
  743.8 7.9 copy.38
  751.7 252.8 %all_to_all.88 = bf16[408,24,384]{2,1,0:T(8,128)(2,1)S(1)} all-to-all(bf16[408,24,384]{2,1,0:T(8,128)(2,1)S(1)} %bitcast.596), channel_id=1, replica_groups=mesh['section'=4,'sp'=8] {'sp'}, dimensions={0} | all-to-all | bytes 15040512 | tf_op jit(solution)/shard_map/all_to_all | solution.py:256
  1021.1 19.2 %convolution_convert_fusion = bf16[48,384,384]{2,1,0:T(8,128)(2,1)} fusion(bf16[48,384,384]{2,1,0:T(8,128)(2,1)} %fusion.186, bf16[48,384,384]{2,1,0:T(8,128)(2,1)} %fusion.307), kind=kOutput, calls=%fused_computation.577 | convolution fusion | flops 5442895872 | bytes 42467328 | tf_op jit(solution)/shard_map/mla,mlk->mak/dot_general | solution.py:274
  1040.3 14.2 fusion.482
  1062.9 6.3 copy.70
  1069.2 72.0 %all-to-all-done.5 = bf16[48,96,384]{2,0,1:T(8,128)(2,1)} async-done(((bf16[48,96,384]{2,0,1:T(8,128)(2,1)}), bf16[48,96,384]{2,0,1:T(8,128)(2,1)}, u32[]{:S(2)}, u32[]{:S(2)}) %all-to-all-start.5) | async-done | bytes 3538976 | tf_op jit(solution)/shard_map/all_to_all | solution.py:281
  1146.1 6.3 copy.73
  1152.4 71.9 %all-to-all-done.3 = bf16[48,96,384]{2,0,1:T(8,128)(2,1)} async-done(((bf16[48,96,384]{2,0,1:T(8,128)(2,1)}), bf16[48,96,384]{2,0,1:T(8,128)(2,1)}, u32[]{:S(2)}, u32[]{:S(2)}) %all-to-all-start.3) | async-done | bytes 3538976 | tf_op jit(solution)/shard_map/all_to_all | solution.py:281
  1228.8 6.2 copy.71
  1235.0 72.4 %all-to-all-done.6 = bf16[48,96,384]{2,0,1:T(8,128)(2,1)} async-done(((bf16[48,96,384]{2,0,1:T(8,128)(2,1)}), bf16[48,96,384]{2,0,1:T(8,128)(2,1)}, u32[]{:S(2)}, u32[]{:S(2)}) %all-to-all-start.6) | async-done | bytes 3538976 | tf_op jit(solution)/shard_map/all_to_all | solution.py:281
  1312.1 5.5 multiply_convert_fusion.10
  1317.6 9.5 copy.61
  1327.2 12.9 reshape.7129
  1340.1 9.5 copy.58
  1349.7 13.0 reshape.7126
  1362.6 9.5 copy.60
  1372.1 13.1 reshape.7128
  1385.2 6.2 fusion.483
  1396.1 5.1 fusion.484
  1405.7 5.1 fusion.485
  1413.7 9.5 copy.59
  1423.2 13.1 reshape.7127
  1436.4 6.2 fusion.486
  1446.2 6.9 fusion.264
  1453.0 6.5 fusion.265
  1459.6 6.9 fusion.266
  1466.4 32.9 %fusion.251 = (u16[768,384]{1,0:T(8,128)(2,1)S(1)}, u16[768,384]{1,0:T(8,128)(2,1)S(1)}, u16[768,384]{1,0:T(8,128)(2,1)S(1)}, u16[768,384]{1,0:T(8,128)(2,1)S(1)...) fusion(f32[384]{0:T(512)S(1)} %convert_reduce_fusion.1, ...), kind=kOutput, calls=%fused_computation.617 | convolution fusion | flops 1561853952 | bytes 68643072 | tf_op jit(solution)/shard_map/acn,ch->anh/dot_general | solution.py:296
  1499.3 37.1 %fusion.246 = bf16[12,192,768]{2,1,0:T(8,128)(2,1)} fusion(f32[12,192,768]{2,1,0:T(8,128)} %copy-done.21, f32[12,768,384]{2,1,0:T(8,128)} %get-tuple-element.1155, f32[384]{0:T(512)S(1)} %convert_reduce_fusion.1, u16[768,384]{1,0:T(8,128)(2,1)S(1)} %get-tuple-element.775, u16[768,384]{1,0:T(8,128)(2,1)S(1)} %get-tuple-element.774, ...), kind=kOutput, calls=%fused_computation.603 | convolution fusion | flops 1613758464 | bytes 26101248 | tf_op jit(solution)/shard_map/anh,ch->acn/dot_general | solution.py:300
  1536.5 37.0 %fusion.243 = bf16[12,192,768]{2,1,0:T(8,128)(2,1)} fusion(f32[12,192,768]{2,1,0:T(8,128)} %copy-done.8, f32[12,768,384]{2,1,0:T(8,128)S(1)} %copy-done.18, f32[384]{0:T(512)S(1)} %convert_reduce_fusion.1, u16[768,384]{1,0:T(8,128)(2,1)S(1)} %get-tuple-element.782, u16[768,384]{1,0:T(8,128)(2,1)S(1)} %get-tuple-element.783, ...), kind=kOutput, calls=%fused_computation.597 | convolution fusion | flops 1613758464 | bytes 26101248 | tf_op jit(solution)/shard_map/anh,ch->acn/dot_general | solution.py:300
  1575.0 36.2 %fusion.244 = bf16[12,192,768]{2,1,0:T(8,128)(2,1)} fusion(f32[12,192,768]{2,1,0:T(8,128)S(1)} %copy-done.10, f32[12,768,384]{2,1,0:T(8,128)S(1)} %copy-done.17, f32[384]{0:T(512)S(1)} %convert_reduce_fusion.1, u16[768,384]{1,0:T(8,128)(2,1)} %get-tuple-element.784, u16[768,384]{1,0:T(8,128)(2,1)} %get-tuple-element.785, ...), kind=kOutput, calls=%fused_computation.599 | convolution fusion | flops 1613758464 | bytes 26101248 | tf_op jit(solution)/shard_map/anh,ch->acn/dot_general | solution.py:300
  1611.3 33.9 %fusion.245 = bf16[12,192,768]{2,1,0:T(8,128)(2,1)S(1)} fusion(f32[12,192,768]{2,1,0:T(8,128)S(1)} %copy-done.12, f32[12,768,384]{2,1,0:T(8,128)S(1)} %copy-done.16, f32[384]{0:T(512)S(1)} %convert_reduce_fusion.1, u16[768,384]{1,0:T(8,128)(2,1)S(1)} %copy-done.34, u16[768,384]{1,0:T(8,128)(2,1)S(1)} %copy-done.35, bf16[1,192,384]{2,1,0:T(8,128)(2,1)S(1)} %copy-done.32), kind=kOutput, calls=%fused_computation.601 | convolution fusion | flops 1613758464 | bytes 26101248 | tf_op jit(solution)/shard_map/anh,ch->acn/dot_general | solution.py:300
  1645.9 7.5 collective-permute-done.3
  1653.4 37.9 %collective-permute-done.2 = bf16[12,192,768]{2,1,0:T(8,128)(2,1)S(1)} collective-permute-done((bf16[12,192,768]{2,1,0:T(8,128)(2,1)S(1)}, bf16[12,192,768]{2,1,0:T(8,128)(2,1)S(1)}, u32[]{:S(2)}, u32[]{:S(2)}) %collective-permute-start.2) | collective-permute-done | bytes 3538976 | tf_op jit(solution)/shard_map/ppermute | solution.py:21
  1691.3 9.6 maximum_bitcast_fusion
  (438 shorter events, 274.7 us)
Async XLA Ops:
  0.0 1446.2 %copy-start = (bf16[1,192,384]{2,1,0:T(8,128)(2,1)S(1)}, bf16[1,192,384]{2,1,0:T(8,128)(2,1)}, u32[]{:S(2)}) copy-start(bf16[1,192,384]{2,1,0:T(8,128)(2,1)} %param.18) | copy-start | bytes 442372
  0.0 70.3 %copy-start.25 = (s32[384]{0:T(512)}, s32[384]{0:T(512)S(1)}, u32[]{:S(2)}) copy-start(s32[384]{0:T(512)S(1)} %fusion.328) | copy-start | bytes 4612
  62.4 314.1 %all-to-all-start = ((bf16[384,48,384]{2,1,0:T(8,128)(2,1)}), bf16[384,48,384]{2,1,0:T(8,128)(2,1)}, u32[]{:S(2)}, u32[]{:S(2)}) async-start(bf16[384,48,384]{2,1,0:T(8,128)(2,1)} %copy.34), calls=%async_computation | async-start | bytes 28311552 | tf_op jit(solution)/shard_map/all_to_all | solution.py:213
  70.4 1.5 copy-start.28
  71.9 59.7 %copy-start.27 = (f32[384]{0:T(512)S(1)}, f32[384]{0:T(512)}, u32[]{:S(2)}) copy-start(f32[384]{0:T(512)} %sine_log_fusion) | copy-start | bytes 4612
  71.9 59.7 %copy-start.31 = (f32[48]{0:T(128)S(1)}, f32[48]{0:T(128)}, u32[]{:S(2)}) copy-start(f32[48]{0:T(128)} %add_multiply_fusion.16) | copy-start | bytes 580
  71.9 60.4 %copy-start.1 = (f32[24,48,384]{2,1,0:T(8,128)S(1)}, f32[24,48,384]{2,1,0:T(8,128)}, u32[]{:S(2)}) copy-start(f32[24,48,384]{2,1,0:T(8,128)} %custom-call.13) | copy-start | bytes 5308420
  71.9 60.4 %copy-start.19 = (f32[48,384]{1,0:T(8,128)S(1)}, f32[48,384]{1,0:T(8,128)}, u32[]{:S(2)}) copy-start(f32[48,384]{1,0:T(8,128)} %custom-call) | copy-start | bytes 221188
  72.0 60.4 %copy-start.20 = (f32[48,384]{1,0:T(8,128)S(1)}, f32[48,384]{1,0:T(8,128)}, u32[]{:S(2)}) copy-start(f32[48,384]{1,0:T(8,128)} %custom-call.1) | copy-start | bytes 221188
  72.9 2.1 copy-start.2
  72.9 2.1 copy-start.3
  73.0 2.5 copy-start.4
  73.0 3.0 copy-start.5
  87.6 4.4 copy-start.6
  96.6 3.9 copy-start.7
  101.5 5.5 copy-start.2
  101.5 5.5 copy-start.3
  101.5 5.5 copy-start.4
  101.5 5.5 copy-start.5
  118.6 4.4 copy-start.6
  127.7 3.9 copy-start.7
  190.4 100.2 %copy-start.24 = (pred[48,384]{1,0:T(8,128)(4,1)S(1)}, pred[48,384]{1,0:T(8,128)(4,1)}, u32[]{:S(2)}) copy-start(pred[48,384]{1,0:T(8,128)(4,1)} %iota_compare_fusion) | copy-start | bytes 55300
  438.5 246.6 %all-to-all-start.1 = ((bf16[408,24,384]{2,1,0:T(8,128)(2,1)}), bf16[408,24,384]{2,1,0:T(8,128)(2,1)}, u32[]{:S(2)}, u32[]{:S(2)}) async-start(bf16[408,24,384]{2,1,0:T(8,128)(2,1)} %slice_dynamic-update-slice_fusion.1), calls=%async_computation.1 | async-start | bytes 15040512 | tf_op jit(solution)/shard_map/all_to_all | solution.py:233
  443.4 8.8 copy-start.33
  447.5 197.0 %collective-permute-start = (bf16[24,192,384]{2,1,0:T(8,128)(2,1)}, bf16[24,192,384]{2,1,0:T(8,128)(2,1)}, u32[]{:S(2)}, u32[]{:S(2)}) collective-permute-start(bf16[24,192,384]{2,1,0:T(8,128)(2,1)} %slice_bitcast_fusion), channel_id=1, source_target_pairs={{0,7},{1,6},{2,5},{3,4},{4,3},{5,2},{6,1},{7,0},{8,15},{9,14},{10,... | collective-permute-start | bytes 10616840 | tf_op jit(solution)/shard_map/ppermute | solution.py:220
  648.0 1.8 copy-start.13
  648.0 2.9 copy-start.15
  721.2 3.1 copy-start.14
  1058.4 82.8 %all-to-all-start.5 = ((bf16[48,96,384]{2,0,1:T(8,128)(2,1)}), bf16[48,96,384]{2,0,1:T(8,128)(2,1)}, u32[]{:S(2)}, u32[]{:S(2)}) async-start(bf16[48,96,384]{2,0,1:T(8,128)(2,1)} %bitcast.605), calls=%async_computation.5 | async-start | bytes 7077888 | tf_op jit(solution)/shard_map/all_to_all | solution.py:281
  1141.2 83.0 %all-to-all-start.3 = ((bf16[48,96,384]{2,0,1:T(8,128)(2,1)}), bf16[48,96,384]{2,0,1:T(8,128)(2,1)}, u32[]{:S(2)}, u32[]{:S(2)}) async-start(bf16[48,96,384]{2,0,1:T(8,128)(2,1)} %bitcast.604), calls=%async_computation.3 | async-start | bytes 7077888 | tf_op jit(solution)/shard_map/all_to_all | solution.py:281
  1224.2 83.1 %all-to-all-start.6 = ((bf16[48,96,384]{2,0,1:T(8,128)(2,1)}), bf16[48,96,384]{2,0,1:T(8,128)(2,1)}, u32[]{:S(2)}, u32[]{:S(2)}) async-start(bf16[48,96,384]{2,0,1:T(8,128)(2,1)} %bitcast.603), calls=%async_computation.6 | async-start | bytes 7077888 | tf_op jit(solution)/shard_map/all_to_all | solution.py:281
  1307.4 4.7 copy-start.30
  1307.4 4.7 copy-start.29
  1307.4 4.7 copy-start.26
  1307.4 106.3 %all-to-all-start.4 = ((bf16[48,96,384]{2,0,1:T(8,128)(2,1)}), bf16[48,96,384]{2,0,1:T(8,128)(2,1)}, u32[]{:S(2)}, u32[]{:S(2)}) async-start(bf16[48,96,384]{2,0,1:T(8,128)(2,1)} %bitcast.602), calls=%async_computation.4 | async-start | bytes 7077888 | tf_op jit(solution)/shard_map/all_to_all | solution.py:281
  1391.5 3.6 copy-start.8
  1391.5 4.6 copy-start.23
  1401.2 3.6 copy-start.21
  1401.2 4.6 copy-start.22
  1410.8 2.8 copy-start.9
  1442.6 3.6 copy-start.11
  1442.6 10.4 slice-start.2
  1446.2 6.9 slice-start.3
  1446.2 13.4 slice-start
  1453.0 6.5 slice-start.1
  1466.4 32.9 %copy-start.32 = (bf16[1,192,384]{2,1,0:T(8,128)(2,1)S(1)}, bf16[1,192,384]{2,1,0:T(8,128)(2,1)}, u32[]{:S(2)}) copy-start(bf16[1,192,384]{2,1,0:T(8,128)(2,1)} %param.20) | copy-start | bytes 442372
  1499.3 37.1 %copy-start.18 = (f32[12,768,384]{2,1,0:T(8,128)S(1)}, f32[12,768,384]{2,1,0:T(8,128)}, u32[]{:S(2)}) copy-start(f32[12,768,384]{2,1,0:T(8,128)} %fusion.266) | copy-start | bytes 42467332
  1536.4 109.5 %collective-permute-start.1 = (bf16[12,192,768]{2,1,0:T(8,128)(2,1)}, bf16[12,192,768]{2,1,0:T(8,128)(2,1)}, u32[]{:S(2)}, u32[]{:S(2)}) collective-permute-start(bf16[12,192,768]{2,1,0:T(8,128)(2,1)} %fusion.246), channel_id=1, source_target_pairs={{0,8},{8,16},{16,24},{24,0},{1,9},{9,17},{17,25},{25,1},{2,10},{10... | collective-permute-start | bytes 10616840 | tf_op jit(solution)/shard_map/ppermute | solution.py:21
  1536.4 38.6 %copy-start.10 = (f32[12,192,768]{2,1,0:T(8,128)S(1)}, f32[12,192,768]{2,1,0:T(8,128)}, u32[]{:S(2)}) copy-start(f32[12,192,768]{2,1,0:T(8,128)} %copy-done.9) | copy-start | bytes 21233668
  1536.4 38.6 %copy-start.17 = (f32[12,768,384]{2,1,0:T(8,128)S(1)}, f32[12,768,384]{2,1,0:T(8,128)}, u32[]{:S(2)}) copy-start(f32[12,768,384]{2,1,0:T(8,128)} %fusion.265) | copy-start | bytes 42467332
  1573.4 72.5 %collective-permute-start.4 = (bf16[12,192,768]{2,1,0:T(8,128)(2,1)}, bf16[12,192,768]{2,1,0:T(8,128)(2,1)}, u32[]{:S(2)}, u32[]{:S(2)}) collective-permute-start(bf16[12,192,768]{2,1,0:T(8,128)(2,1)} %fusion.243), channel_id=1, source_target_pairs={{0,8},{8,16},{16,24},{24,0},{1,9},{9,17},{17,25},{25,1},{2,10},{10... | collective-permute-start | bytes 10616840 | tf_op jit(solution)/shard_map/ppermute | solution.py:21
  1575.0 36.3 %copy-start.12 = (f32[12,192,768]{2,1,0:T(8,128)S(1)}, f32[12,192,768]{2,1,0:T(8,128)}, u32[]{:S(2)}) copy-start(f32[12,192,768]{2,1,0:T(8,128)} %copy-done.11) | copy-start | bytes 21233668
  1575.0 36.3 %copy-start.16 = (f32[12,768,384]{2,1,0:T(8,128)S(1)}, f32[12,768,384]{2,1,0:T(8,128)}, u32[]{:S(2)}) copy-start(f32[12,768,384]{2,1,0:T(8,128)} %fusion.264) | copy-start | bytes 42467332
  1575.0 36.3 %copy-start.34 = (u16[768,384]{1,0:T(8,128)(2,1)S(1)}, u16[768,384]{1,0:T(8,128)(2,1)}, u32[]{:S(2)}) copy-start(u16[768,384]{1,0:T(8,128)(2,1)} %get-tuple-element.786) | copy-start | bytes 1769476
  1575.0 36.3 %copy-start.35 = (u16[768,384]{1,0:T(8,128)(2,1)S(1)}, u16[768,384]{1,0:T(8,128)(2,1)}, u32[]{:S(2)}) copy-start(u16[768,384]{1,0:T(8,128)(2,1)} %get-tuple-element.787) | copy-start | bytes 1769476
  1611.3 42.1 %collective-permute-start.3 = (bf16[12,192,768]{2,1,0:T(8,128)(2,1)}, bf16[12,192,768]{2,1,0:T(8,128)(2,1)S(1)}, u32[]{:S(2)}, u32[]{:S(2)}) collective-permute-start(bf16[12,192,768]{2,1,0:T(8,128)(2,1)} %fusion.244), channel_id=1, source_target_pairs={{0,8},{8,16},{16,24},{24,0},{1,9},{9,17},{17,25},{25,1},{2,10},{10... | collective-permute-start | bytes 10616840 | tf_op jit(solution)/shard_map/ppermute | solution.py:21
  1645.2 46.1 %collective-permute-start.2 = (bf16[12,192,768]{2,1,0:T(8,128)(2,1)S(1)}, bf16[12,192,768]{2,1,0:T(8,128)(2,1)S(1)}, u32[]{:S(2)}, u32[]{:S(2)}) collective-permute-start(bf16[12,192,768]{2,1,0:T(8,128)(2,1)S(1)} %fusion.245), channel_id=1, source_target_pairs={{0,8},{8,16},{16,24},{24,0},{1,9},{9,17},{17,25},{25,1},{2,10},{10... | collective-permute-start | bytes 10616840 | tf_op jit(solution)/shard_map/ppermute | solution.py:21
